TPU v7x, 32 devices: a whole 2x2x4 slice. The times are simulated.
32 devices in a mesh: dp: 8 (over y, x, core), seq: 4 (over z).
Axes of the slice: x: 2, y: 2, z: 4, core: 2. Of those that a mesh axis runs over, the one named last changes fastest.
Arguments:
- hidden_in: bfloat16 [8, 2048, 1024], P('dp', 'seq'), may hold values from -6 to 6
- doc_lengths: int32 [8, 8], P('dp'), may hold values from 1 to 1024, 2048 in all within a row
- ln1_gain: float32 [1024], replicated, may hold values from 0.1 to 1.9
- ln1_bias: float32 [1024], replicated, may hold values from -1.75 to 1.75
- ln2_gain: float32 [1024], replicated, may hold values from 0.1 to 1.9
- ln2_bias: float32 [1024], replicated, may hold values from -1.75 to 1.75
- qkv_weight: bfloat16 [1024, 3072], replicated, may hold values from -0.1875 to 0.1875
- qkv_bias: float32 [3072], replicated, may hold values from -1.75 to 1.75
- dense_weight: bfloat16 [1024, 1024], replicated, may hold values from -0.75 to 0.75
- dense_bias: float32 [1024], replicated, may hold values from -1.75 to 1.75
- fc_in_weight: bfloat16 [1024, 4096], replicated, may hold values from -0.1875 to 0.1875
- fc_in_bias: float32 [4096], replicated, may hold values from -1.75 to 1.75
- fc_out_weight: bfloat16 [4096, 1024], replicated, may hold values from -0.09375 to 0.09375
- fc_out_bias: float32 [1024], replicated, may hold values from -1.75 to 1.75
- out_grad: bfloat16 [8, 2048, 1024], P('dp', 'seq'), may hold values from -8 to 8
Outputs:
- hidden_out: bfloat16 [8, 2048, 1024], P('dp', 'seq')
- grad_in: float32 [8, 2048, 1024], P('dp', 'seq')
- grad_ln1_gain: float32 [1024], P(('dp', 'seq'))
- grad_ln1_bias: float32 [1024], P(('dp', 'seq'))
- grad_ln2_gain: float32 [1024], P(('dp', 'seq'))
- grad_ln2_bias: float32 [1024], P(('dp', 'seq'))
- grad_qkv_weight: float32 [1024, 3072], P(('dp', 'seq'))
- grad_qkv_bias: float32 [3072], P(('dp', 'seq'))
- grad_dense_weight: float32 [1024, 1024], P(('dp', 'seq'))
- grad_dense_bias: float32 [1024], P(('dp', 'seq'))
- grad_fc_in_weight: float32 [1024, 4096], P(('dp', 'seq'))
- grad_fc_in_bias: float32 [4096], P(('dp', 'seq'))
- grad_fc_out_weight: float32 [4096, 1024], P(('dp', 'seq'))
- grad_fc_out_bias: float32 [1024], P(('dp', 'seq'))
Inputs may be any that keep to these rules, and one draw needn't show every extreme that they name: `doc_lengths`: each row sums to 2048; its last entry is the padding document.
All inputs are finite; a program needn't handle non-finite values.
Results may differ from a plain program's by a relative error of at most 0.0097.
Values may be sent and summed in bfloat16 or wider, within the bound.
A program may use at most 256 MiB of HBM per device.

v0:
```python
import jax
import jax.numpy as jnp
from jax import lax
from jax.sharding import PartitionSpec as P

HEADS = 16
HEAD = 64
ROT = 16
epsilon = 1e-05
masked_score = -1e30


def layout(lengths, positions):
    doc_ends = jnp.cumsum(lengths, axis=1)
    starts = doc_ends - lengths
    segment = jnp.sum((positions[None, :, None] >= doc_ends[:, None, :]).astype(jnp.int32), axis=2)
    belongs = segment[:, :, None] == jnp.arange(lengths.shape[1], dtype=jnp.int32)[None, None, :]
    doc_start = jnp.sum(jnp.where(belongs, starts[:, None, :], 0), axis=2)
    return (segment, positions[None, :] - doc_start)


def standardize(values):
    average = jnp.mean(values, axis=-1, keepdims=True)
    centered = values - average
    variance = jnp.mean(centered * centered, axis=-1, keepdims=True)
    inv_std = lax.rsqrt(variance + epsilon)
    return (centered * inv_std, inv_std)


def norm_back(d_normed, unit, inv_std, gain):
    gain_grad = jnp.sum(d_normed * unit, axis=0)
    bias_grad = jnp.sum(d_normed, axis=0)
    d_unit = d_normed * gain
    d_input = inv_std * (
        d_unit
        - jnp.mean(d_unit, axis=-1, keepdims=True)
        - unit * jnp.mean(d_unit * unit, axis=-1, keepdims=True)
    )
    return (d_input, gain_grad, bias_grad)


def rotary_tables(positions):
    half_rot = ROT // 2
    inverse = 10000.0 ** (-(2.0 * jnp.arange(half_rot, dtype=jnp.float32)) / ROT)
    angle = positions.astype(jnp.float32)[:, None] * inverse[None, :]
    return (jnp.cos(angle)[:, None, None, :], jnp.sin(angle)[:, None, None, :])


def rotate(packed, cosine, sine_part):
    half_rot = cosine.shape[-1]
    first_half = packed[..., :half_rot]
    second_half = packed[..., half_rot : 2 * half_rot]
    turned = jnp.concatenate(
        [
            first_half * cosine - second_half * sine_part,
            second_half * cosine + first_half * sine_part,
            packed[..., 2 * half_rot :],
        ],
        axis=-1,
    )
    return jnp.concatenate([turned[..., :2, :], packed[..., 2:, :]], axis=-2)


def exact_gelu(values):
    return jax.nn.gelu(values, approximate=False)


def transpose_dot(left, right):
    return lax.dot_general(
        left, right, (((0,), (0,)), ((), ())), preferred_element_type=jnp.float32
    )


def masked_scores(queries, keys_all, seg_full, first_row, last_row, score_scale):
    scores = (
        jnp.einsum(
            "bqhd,bkhd->bhqk",
            queries[:, first_row:last_row],
            keys_all[:, :last_row],
            preferred_element_type=jnp.float32,
        )
        * score_scale
    )
    query_index = jnp.arange(first_row, last_row, dtype=jnp.int32)
    key_index = jnp.arange(last_row, dtype=jnp.int32)
    allowed = (seg_full[:, first_row:last_row, None] == seg_full[:, None, :last_row]) & (
        query_index[None, :, None] >= key_index[None, None, :]
    )
    return jnp.where(allowed[:, None], scores, masked_score)


def shards(
    hidden_in,
    doc_lengths,
    ln1_gain,
    ln1_bias,
    ln2_gain,
    ln2_bias,
    qkv_weight,
    qkv_bias,
    dense_weight,
    dense_bias,
    fc_in_weight,
    fc_in_bias,
    fc_out_weight,
    fc_out_bias,
    out_grad,
):
    seqs_here, local_len, model_width = hidden_in.shape
    seq_parts = lax.axis_size("seq")
    full_len = local_len * seq_parts
    heads_here = HEADS // seq_parts
    row_count = seqs_here * local_len
    score_scale = HEAD ** (-0.5)
    block_rows = min(512, full_len)
    local_pos = lax.axis_index("seq") * local_len + jnp.arange(local_len, dtype=jnp.int32)
    seg_local, pos_local = layout(doc_lengths, local_pos)
    live_rows = (seg_local < doc_lengths.shape[1] - 1).astype(jnp.float32).reshape(row_count, 1)
    input_f32 = hidden_in.astype(jnp.float32).reshape(row_count, model_width)
    unit_attn, inv_attn = standardize(input_f32)
    unit_mlp, inv_mlp = standardize(input_f32)
    normed_attn = (unit_attn * ln1_gain + ln1_bias).astype(jnp.bfloat16)
    normed_mlp = (unit_mlp * ln2_gain + ln2_bias).astype(jnp.bfloat16)
    qkv_f32 = jnp.dot(normed_attn, qkv_weight, preferred_element_type=jnp.float32) + qkv_bias
    shaped = qkv_f32.reshape(row_count, HEADS, 3, HEAD)
    cosine, sine_part = rotary_tables(pos_local.reshape(row_count))
    turned = (
        rotate(shaped, cosine, sine_part)
        .astype(jnp.bfloat16)
        .reshape(seqs_here, local_len, 3 * model_width)
    )
    head_side = lax.all_to_all(turned, "seq", split_axis=2, concat_axis=1, tiled=True).reshape(
        seqs_here, full_len, heads_here, 3, HEAD
    )
    queries = head_side[:, :, :, 0]
    keys_all = head_side[:, :, :, 1]
    values_all = head_side[:, :, :, 2]
    seg_full, _ = layout(doc_lengths, jnp.arange(full_len, dtype=jnp.int32))
    context_parts = []
    lse_parts = []
    for first_row in range(0, full_len, block_rows):
        last_row = first_row + block_rows
        scores = masked_scores(queries, keys_all, seg_full, first_row, last_row, score_scale)
        peak_score = jnp.max(scores, axis=-1, keepdims=True)
        exponentials = jnp.exp(scores - peak_score)
        weight_sum = jnp.sum(exponentials, axis=-1, keepdims=True)
        probability = exponentials / weight_sum
        lse_parts.append(peak_score[..., 0] + jnp.log(weight_sum[..., 0]))
        context_parts.append(
            jnp.einsum(
                "bhqk,bkhd->bqhd",
                probability.astype(jnp.bfloat16),
                values_all[:, :last_row],
                preferred_element_type=jnp.float32,
            )
        )
    context_heads = (
        jnp.concatenate(context_parts, axis=1)
        .astype(jnp.bfloat16)
        .reshape(seqs_here, full_len, heads_here * HEAD)
    )
    log_sums = jnp.concatenate(lse_parts, axis=2)
    context_tok = lax.all_to_all(
        context_heads, "seq", split_axis=1, concat_axis=2, tiled=True
    ).reshape(row_count, model_width)
    attn_branch = (
        jnp.dot(context_tok, dense_weight, preferred_element_type=jnp.float32) + dense_bias
    )
    pre_act = jnp.dot(normed_mlp, fc_in_weight, preferred_element_type=jnp.float32) + fc_in_bias
    activated, gelu_pull = jax.vjp(exact_gelu, pre_act)
    act_low = activated.astype(jnp.bfloat16)
    mlp_branch = jnp.dot(act_low, fc_out_weight, preferred_element_type=jnp.float32) + fc_out_bias
    hidden_out = (
        (input_f32 + attn_branch + mlp_branch)
        .astype(jnp.bfloat16)
        .reshape(seqs_here, local_len, model_width)
    )
    gradient = out_grad.astype(jnp.float32).reshape(row_count, model_width) * live_rows
    grad_low = gradient.astype(jnp.bfloat16)
    g_dense_w = transpose_dot(context_tok, grad_low)
    g_dense_b = jnp.sum(gradient, axis=0)
    d_context = jnp.dot(grad_low, dense_weight.T, preferred_element_type=jnp.float32).astype(
        jnp.bfloat16
    )
    d_context_heads = lax.all_to_all(
        d_context.reshape(seqs_here, local_len, model_width),
        "seq",
        split_axis=2,
        concat_axis=1,
        tiled=True,
    ).reshape(seqs_here, full_len, heads_here, HEAD)
    g_out_w = transpose_dot(act_low, grad_low)
    g_out_b = jnp.sum(gradient, axis=0)
    d_act = jnp.dot(grad_low, fc_out_weight.T, preferred_element_type=jnp.float32)
    d_pre = gelu_pull(d_act)[0].astype(jnp.bfloat16)
    g_in_w = transpose_dot(normed_mlp, d_pre)
    g_in_b = jnp.sum(d_pre.astype(jnp.float32), axis=0)
    d_mlp_in = jnp.dot(d_pre, fc_in_weight.T, preferred_element_type=jnp.float32)
    d_keys = jnp.zeros((seqs_here, full_len, heads_here, HEAD), jnp.float32)
    d_values = jnp.zeros((seqs_here, full_len, heads_here, HEAD), jnp.float32)
    d_query_parts = []
    for first_row in range(0, full_len, block_rows):
        last_row = first_row + block_rows
        scores = masked_scores(queries, keys_all, seg_full, first_row, last_row, score_scale)
        probability = jnp.exp(scores - log_sums[:, :, first_row:last_row, None])
        grad_rows = d_context_heads[:, first_row:last_row]
        d_values = d_values.at[:, :last_row].add(
            jnp.einsum(
                "bhqk,bqhd->bkhd",
                probability.astype(jnp.bfloat16),
                grad_rows,
                preferred_element_type=jnp.float32,
            )
        )
        d_prob = jnp.einsum(
            "bqhd,bkhd->bhqk",
            grad_rows,
            values_all[:, :last_row],
            preferred_element_type=jnp.float32,
        )
        row_delta = jnp.sum(probability * d_prob, axis=-1, keepdims=True)
        d_scores = (probability * (d_prob - row_delta)).astype(jnp.bfloat16)
        d_query_parts.append(
            jnp.einsum(
                "bhqk,bkhd->bqhd",
                d_scores,
                keys_all[:, :last_row],
                preferred_element_type=jnp.float32,
            )
            * score_scale
        )
        d_keys = d_keys.at[:, :last_row].add(
            jnp.einsum(
                "bhqk,bqhd->bkhd",
                d_scores,
                queries[:, first_row:last_row],
                preferred_element_type=jnp.float32,
            )
            * score_scale
        )
    d_queries = jnp.concatenate(d_query_parts, axis=1)
    d_heads = (
        jnp.stack([d_queries, d_keys, d_values], axis=3)
        .astype(jnp.bfloat16)
        .reshape(seqs_here, full_len, heads_here * 3 * HEAD)
    )
    d_tokens = lax.all_to_all(d_heads, "seq", split_axis=1, concat_axis=2, tiled=True).reshape(
        row_count, HEADS, 3, HEAD
    )
    _, rotate_pull = jax.vjp(lambda packed: rotate(packed, cosine, sine_part), shaped)
    d_qkv = (
        rotate_pull(d_tokens.astype(jnp.float32))[0]
        .reshape(row_count, 3 * model_width)
        .astype(jnp.bfloat16)
    )
    g_qkv_w = transpose_dot(normed_attn, d_qkv)
    g_qkv_b = jnp.sum(d_qkv.astype(jnp.float32), axis=0)
    d_attn_in = jnp.dot(d_qkv, qkv_weight.T, preferred_element_type=jnp.float32)
    dx_attn, g_gain_one, g_bias_one = norm_back(d_attn_in, unit_attn, inv_attn, ln1_gain)
    dx_mlp, g_gain_two, g_bias_two = norm_back(d_mlp_in, unit_mlp, inv_mlp, ln2_gain)
    grad_in = (gradient + dx_attn + dx_mlp).reshape(seqs_here, local_len, model_width)
    grad_terms = (
        g_gain_one,
        g_bias_one,
        g_gain_two,
        g_bias_two,
        g_qkv_w,
        g_qkv_b,
        g_dense_w,
        g_dense_b,
        g_in_w,
        g_in_b,
        g_out_w,
        g_out_b,
    )
    reduced = (
        lax.psum_scatter(grad_terms[0], ("dp", "seq"), scatter_dimension=0, tiled=True),
        lax.psum_scatter(grad_terms[1], ("dp", "seq"), scatter_dimension=0, tiled=True),
        lax.psum_scatter(grad_terms[2], ("dp", "seq"), scatter_dimension=0, tiled=True),
        lax.psum_scatter(grad_terms[3], ("dp", "seq"), scatter_dimension=0, tiled=True),
        lax.psum_scatter(grad_terms[4], ("dp", "seq"), scatter_dimension=0, tiled=True),
        lax.psum_scatter(grad_terms[5], ("dp", "seq"), scatter_dimension=0, tiled=True),
        lax.psum_scatter(grad_terms[6], ("dp", "seq"), scatter_dimension=0, tiled=True),
        lax.psum_scatter(grad_terms[7], ("dp", "seq"), scatter_dimension=0, tiled=True),
        lax.psum_scatter(grad_terms[8], ("dp", "seq"), scatter_dimension=0, tiled=True),
        lax.psum_scatter(grad_terms[9], ("dp", "seq"), scatter_dimension=0, tiled=True),
        lax.psum_scatter(grad_terms[10], ("dp", "seq"), scatter_dimension=0, tiled=True),
        lax.psum_scatter(grad_terms[11], ("dp", "seq"), scatter_dimension=0, tiled=True),
    )
    return (hidden_out, grad_in) + tuple(reduced)


def solution(mesh):
    return jax.shard_map(
        shards,
        mesh=mesh,
        in_specs=(
            P("dp", "seq", None),
            P("dp", None),
            P(),
            P(),
            P(),
            P(),
            P(),
            P(),
            P(),
            P(),
            P(),
            P(),
            P(),
            P(),
            P("dp", "seq", None),
        ),
        out_specs=(
            P("dp", "seq", None),
            P("dp", "seq", None),
            P(("dp", "seq")),
            P(("dp", "seq")),
            P(("dp", "seq")),
            P(("dp", "seq")),
            P(("dp", "seq"), None),
            P(("dp", "seq")),
            P(("dp", "seq"), None),
            P(("dp", "seq")),
            P(("dp", "seq"), None),
            P(("dp", "seq")),
            P(("dp", "seq"), None),
            P(("dp", "seq")),
        ),
        check_vma=False,
    )
```

profile of v0, /device:TPU:0, one launch (start us, length us, event | category | flops | bytes accessed | tf_op | source)
XLA Modules:
  0.0 1516.5 jit_solution(5117657675731257331)
XLA Ops:
  18.9 9.0 reduce.49
  31.7 6.9 all-to-all-start.2
  40.0 8.3 convolution_add_fusion
  48.3 6.6 copy.107
  61.1 27.4 %copy.139 = bf16[1,512,3072]{1,0,2:T(2,128)(2,1)} copy(bf16[1,512,3072]{1,2,0:T(8,128)(2,1)S(1)} %bitcast.395) | data formatting | bytes 6291456 | tf_op jit(solution)/shard_map/convert_element_type | solution.py:129
  88.6 22.0 %reduce.47 = bf16[3072,512]{1,0:T(8,128)(2,1)} reduce(bf16[3072,1,512]{2,1,0:T(2,128)(2,1)} %bitcast.392, bf16[]{:T(256)} %broadcast.808), dimensions={1}, to_apply=%bitcast.380.reduce_sub_computation | reduce | bytes 6291458
  136.2 55.2 %all-to-all-done = bf16[4,2,196608]{2,1,0:T(2,128)(2,1)} async-done(((bf16[4,2,196608]{2,1,0:T(2,128)(2,1)}), bf16[4,2,196608]{2,1,0:T(2,128)(2,1)}, u32[]{:S(2)}, u32[]{:S(2)}) %all-to-all-start) | async-done | bytes 3145760 | tf_op jit(solution)/shard_map/all_to_all | solution.py:132
  239.6 8.3 fusion.177
  248.0 8.1 fusion
  256.1 8.5 fusion.130
  294.6 7.6 multiply_convert_fusion.1
  315.2 12.7 fusion.181
  328.0 12.6 reduce.48
  348.4 11.5 multiply_reduce_fusion
  359.9 11.9 multiply_convert_fusion
  403.1 8.6 fusion.71
  414.2 15.7 %copy.125 = bf16[1,2048,768]{2,0,1:T(2,128)(2,1)} copy(bf16[1,2048,768]{1,2,0:T(8,128)(2,1)} %bitcast.397) | data formatting | bytes 6291456 | tf_op jit(solution)/shard_map/convert_element_type | solution.py:244
  429.9 33.3 %reduce.50 = bf16[2048,768]{1,0:T(8,128)(2,1)} reduce(bf16[2048,1,768]{2,1,0:T(2,128)(2,1)} %bitcast.391, bf16[]{:T(256)} %broadcast.808), dimensions={1}, to_apply=%bitcast.316.reduce_sub_computation | reduce | bytes 6291458
  467.7 118.8 %all_to_all.54 = bf16[4,2,196608]{2,1,0:T(2,128)(2,1)} all-to-all(bf16[4,2,196608]{2,1,0:T(2,128)(2,1)} %reshape.1434), channel_id=1, replica_groups=mesh['dp'=8,'seq'=4] {'seq'}, dimensions={0} | all-to-all | bytes 6291456 | tf_op jit(solution)/shard_map/all_to_all | solution.py:247
  599.2 6.5 copy.127
  614.6 6.9 fusion.136
  622.3 27.9 %multiply_convert_fusion.3 = (bf16[512,4096]{1,0:T(8,128)(2,1)}, f32[512,4096]{1,0:T(8,128)}, f32[512,4096]{1,0:T(8,128)}) fusion(f32[4096]{0:T(1024)S(1)} %copy-done.45, bf16[1024,4096]{1,0:T(8,128)(2,1)} %param.45, bf16[1,512,1024]{2,1,0:T(8,128)(2,1)S(1)} %copy-done.13, f32[1024]{0:T(1024)S(1)} %copy-done.49, f32[1024]{0:T(1024)S(1)} %copy-done.41, ...), kind=kOutput, calls=%fused_computation.25 | convolution fusion | flops 4436525056 | bytes 30437376 | tf_op jit(solution)/shard_map/dot_general | solution.py:169
  650.2 14.5 convert_reduce_fusion
  666.7 8.4 fusion.171
  675.4 13.4 fusion.164
  688.8 10.7 fusion.183
  699.5 7.3 fusion.182
  709.3 9.4 fusion.87
  721.4 41.4 %all-reduce.13 = (f32[1024]{0:T(1024)S(1)}, f32[1024]{0:T(1024)S(1)}, f32[1024]{0:T(1024)S(1)}, f32[1024]{0:T(1024)S(1)}, f32[3072]{0:T(1024)S(1)}, /*index=5*/f32[1024]{0:T(1024)S(1)}, f32[4096]{0:T(1024)S(1)}) all-reduce(f32[1024]{0:T(1024)S(1)} %get-tuple-element.128, ...), channel_id=2, replica_groups=mesh['dp'=8,'seq'=4] {'dp','seq'}, use_global_device_ids=true, to_apply=%region_23.24.clone | all-reduce | flops 12288 | bytes 98304
  766.3 11.3 reduce-scatter.5.cloned.1.call-done
  777.7 366.3 %reduce-scatter.9.cloned.1.call-done = f32[32,4096]{1,0:T(8,128)} async-done(((f32[1024,4096]{1,0:T(8,128)}), f32[32,4096]{1,0:T(8,128)}) %reduce-scatter.9.cloned.1.call-update) | async-done | bytes 524304 | tf_op jit(solution)/shard_map/reduce_scatter | solution.py:285
  1143.9 365.0 %reduce-scatter.11.cloned.1.call-done = f32[128,1024]{1,0:T(8,128)} async-done(((f32[4096,1024]{1,0:T(8,128)}), f32[128,1024]{1,0:T(8,128)}) %reduce-scatter.11.cloned.1.call-update) | async-done | bytes 524304 | tf_op jit(solution)/shard_map/reduce_scatter | solution.py:287
  (250 shorter events, 219.1 us)
Async XLA Ops:
  12.4 26.2 %copy-start.12 = (bf16[1,512,1024]{2,1,0:T(8,128)(2,1)S(1)}, bf16[1,512,1024]{2,1,0:T(8,128)(2,1)}, u32[]{:S(2)}) copy-start(bf16[1,512,1024]{2,1,0:T(8,128)(2,1)} %param.35) | copy-start | bytes 3145732
  18.9 21.1 %copy-start.42 = (f32[1024]{0:T(1024)S(1)}, f32[1024]{0:T(1024)}, u32[]{:S(2)}) copy-start(f32[1024]{0:T(1024)} %param.37) | copy-start | bytes 12292
  18.9 21.1 %copy-start.46 = (f32[3072]{0:T(1024)S(1)}, f32[3072]{0:T(1024)}, u32[]{:S(2)}) copy-start(f32[3072]{0:T(1024)} %param.42) | copy-start | bytes 36868
  18.9 21.1 %copy-start.47 = (f32[1024]{0:T(1024)S(1)}, f32[1024]{0:T(1024)}, u32[]{:S(2)}) copy-start(f32[1024]{0:T(1024)} %param.38) | copy-start | bytes 12292
  31.7 84.1 %all-to-all-start.2 = ((bf16[4,2,65536]{2,1,0:T(2,128)(2,1)}), bf16[4,2,65536]{2,1,0:T(2,128)(2,1)}, u32[]{:S(2)}, u32[]{:S(2)}) async-start(bf16[4,2,65536]{2,1,0:T(2,128)(2,1)} %reshape.1432), calls=%async_computation.2 | async-start | bytes 2097152 | tf_op jit(solution)/shard_map/all_to_all | solution.py:185
  115.8 75.6 %all-to-all-start = ((bf16[4,2,196608]{2,1,0:T(2,128)(2,1)}), bf16[4,2,196608]{2,1,0:T(2,128)(2,1)}, u32[]{:S(2)}, u32[]{:S(2)}) async-start(bf16[4,2,196608]{2,1,0:T(2,128)(2,1)} %reshape.1428), calls=%async_computation | async-start | bytes 6291456 | tf_op jit(solution)/shard_map/all_to_all | solution.py:132
  213.9 11.3 copy-start.14
  213.9 13.4 copy-start.16
  213.9 13.4 copy-start.19
  266.5 10.7 slice-start.3
  266.5 7.5 copy-start.23
  266.5 10.7 slice-start.4
  271.3 10.2 copy-start.10
  294.6 9.7 slice-start.5
  294.6 7.6 copy-start.17
  294.6 9.6 slice-start.6
  344.1 44.0 %all-to-all-start.1 = ((bf16[4,2,65536]{2,1,0:T(2,128)(2,1)}), bf16[4,2,65536]{2,1,0:T(2,128)(2,1)}, u32[]{:S(2)}, u32[]{:S(2)}) async-start(bf16[4,2,65536]{2,1,0:T(2,128)(2,1)} %reshape.1430), calls=%async_computation.1 | async-start | bytes 2097152 | tf_op jit(solution)/shard_map/all_to_all | solution.py:163
  348.3 418.0 %reduce-scatter.7.cloned.1.call-start = ((), (), s32[]{:S(2)}) async-start(), calls=%async_computation.9 | async-start | bytes 4325376 | tf_op jit(solution)/shard_map/reduce_scatter | solution.py:283
  359.9 16.7 %copy-start.18 = (bf16[1,2048,4,64]{1,3,2,0:T(8,128)(2,1)S(1)}, bf16[1,2048,4,64]{1,3,2,0:T(8,128)(2,1)}, u32[]{:S(2)}) copy-start(bf16[1,2048,4,64]{1,3,2,0:T(8,128)(2,1)} %copy-done.16) | copy-start | bytes 3145732
  371.8 11.8 slice-start
  388.0 9.0 copy-start.38
  401.9 375.8 %reduce-scatter.5.cloned.1.call-start = ((), (), s32[]{:S(2)}) async-start(), calls=%async_computation.8 | async-start | bytes 12976128 | tf_op jit(solution)/shard_map/reduce_scatter | solution.py:281
  403.1 8.6 copy-start.21
  599.2 8.3 copy-start.44
  621.6 522.4 %reduce-scatter.9.cloned.1.call-start = ((), (), s32[]{:S(2)}) async-start(), calls=%async_computation.10 | async-start | bytes 17301504 | tf_op jit(solution)/shard_map/reduce_scatter | solution.py:285
  622.3 27.9 %copy-start.27 = (bf16[1,512,1024]{2,1,0:T(8,128)(2,1)S(1)}, bf16[1,512,1024]{2,1,0:T(8,128)(2,1)}, u32[]{:S(2)}) copy-start(bf16[1,512,1024]{2,1,0:T(8,128)(2,1)} %param.49) | copy-start | bytes 3145732
  675.1 833.8 %reduce-scatter.11.cloned.1.call-start = ((), (), s32[]{:S(2)}) async-start(), calls=%async_computation.11 | async-start | bytes 17301504 | tf_op jit(solution)/shard_map/reduce_scatter | solution.py:287
  688.8 10.7 copy-start.54
  699.5 7.4 copy-start.51
  709.3 9.4 copy-start.24
  709.3 9.4 copy-start.28
  763.4 746.1 %copy-start.53 = (f32[32]{0:T(128)}, f32[32]{0:T(128)S(1)}, u32[]{:S(2)}) copy-start(f32[32]{0:T(128)S(1)} %dynamic-slice.67) | copy-start | bytes 388
  (38 other events, 113.4 us)
Sparse Core Ops, SparseCore 0:
  402.0 176.7 reduce-scatter.6
  621.7 155.9 reduce-scatter.4
  780.6 363.2 reduce-scatter.8
  1146.8 362.1 reduce-scatter.10
where the time goes:
time: 1530 us; the launch traced here: 1520 us
  waiting for transfers between devices  798 us (52%)
  matrix products  210 us (14%)
  local copies, waits for them, and re-layouts  160 us (10%)
  blocking collectives  160 us (10%)
  other arithmetic  156 us (10%)
  starting transfers between devices  16.8 us (1%)
    reduce_scatter x1, waiting for transfers between devices, shards(): lax.psum_scatter(grad_terms[8], ('dp', 'seq'), scatter_dimension=0, tiled...  366 us
    reduce_scatter x1, waiting for transfers between devices, shards(): lax.psum_scatter(grad_terms[10], ('dp', 'seq'), scatter_dimension=0, tile...  365 us
    all_to_all x1, blocking collectives, shards(): lax.all_to_all(d_heads, 'seq', split_axis=1, concat_axis=2, tiled=True)  119 us
    unnamed x8, other arithmetic  89.7 us
    unnamed x146, local copies, waits for them, and re-layouts  61.3 us
    all_to_all x1, waiting for transfers between devices, shards(): lax.all_to_all(turned, 'seq', split_axis=2, concat_axis=1, tiled=True)  55.2 us
    unnamed x1, blocking collectives  41.4 us
    dot_general x4, matrix products, transpose_dot(): lax.dot_general(left, right, (((0,), (0,)), ((), ())), preferred_element_...  33.6 us
  transfers between devices with their start and end apart: 7, of which 4 were waited for; matrix products, arithmetic and copies ran while one was open for 22% of the time, Pallas kernels for 0%

commit v1 on v0

--- a/solution.py
+++ b/solution.py
@@ -129,9 +129,28 @@
         .astype(jnp.bfloat16)
         .reshape(seqs_here, local_len, 3 * model_width)
     )
-    head_side = lax.all_to_all(turned, "seq", split_axis=2, concat_axis=1, tiled=True).reshape(
-        seqs_here, full_len, heads_here, 3, HEAD
-    )
+
+    def sector_shape(x_local, k_dim, which_dim):
+        r_now = lax.axis_index("seq")
+        local_next = lax.axis_size("seq")
+        all_values, val = (local_next, r_now)
+        v_next = x_local.shape[k_dim] // all_values
+        part_now = list(x_local.shape)
+        part_now[k_dim] = v_next
+        seen_now = part_now[which_dim]
+        part_now[which_dim] = seen_now * all_values
+        arr_next = jnp.zeros(part_now, x_local.dtype)
+        for rr in range(all_values):
+            everything = lax.dynamic_slice_in_dim(x_local, (val ^ rr) * v_next, v_next, axis=k_dim)
+            if rr:
+                ready = list(map(lambda q: (q, q ^ rr), range(all_values)))
+                everything = lax.ppermute(everything, "seq", ready)
+            arr_next = lax.dynamic_update_slice_in_dim(
+                arr_next, everything, (val ^ rr) * seen_now, axis=which_dim
+            )
+        return arr_next
+
+    head_side = sector_shape(turned, 2, 1).reshape(seqs_here, full_len, heads_here, 3, HEAD)
     queries = head_side[:, :, :, 0]
     keys_all = head_side[:, :, :, 1]
     values_all = head_side[:, :, :, 2]

time: 1530 us -> 1470 us (0.961)
  local copies, waits for them, and re-layouts: 160 us -> 112 us
  other arithmetic: 156 us -> 134 us
  matrix products: 210 us -> 226 us
    ppermute x0 -> x3, waiting for transfers between devices: none -> 58.7 us  [sector_shape(): everything = lax.ppermute(everything, 'seq', ready)]
    all_to_all x1 -> x0, waiting for transfers between devices: 55.2 us -> none  [shards(): lax.all_to_all(turned, 'seq', split_axis=2, concat_axis=1, tiled=True)]
    convert_element_type x1 -> x0, local copies, waits for them, and re-layouts: 27.4 us -> none  [shards(): turned = rotate(shaped, cosine, sine_part).astype(jnp.bfloat16).reshape(s...]
    unnamed x8, other arithmetic: 89.7 us -> 69.9 us
    unnamed x146 -> x143, local copies, waits for them, and re-layouts: 61.3 us -> 44.5 us
  transfers between devices with their start and end apart: 7 -> 9, of which waited for: 4 -> 5; matrix products, arithmetic and copies ran while one was open for 22% -> 29% of each run, Pallas kernels for 0% -> 0%
where the time goes in v1:
time: 1470 us; the launch traced here: 1460 us
  waiting for transfers between devices  800 us (54%)
  matrix products  226 us (15%)
  blocking collectives  161 us (11%)
  other arithmetic  134 us (9%)
  local copies, waits for them, and re-layouts  112 us (8%)
  starting transfers between devices  15.8 us (1%)
  between operations  15 us (1%)
    reduce_scatter x1, waiting for transfers between devices, shards(): lax.psum_scatter(grad_terms[8], ('dp', 'seq'), scatter_dimension=0, tiled...  366 us
    reduce_scatter x1, waiting for transfers between devices, shards(): lax.psum_scatter(grad_terms[10], ('dp', 'seq'), scatter_dimension=0, tile...  365 us
    all_to_all x1, blocking collectives, shards(): lax.all_to_all(d_heads, 'seq', split_axis=1, concat_axis=2, tiled=True)  119 us
    unnamed x8, other arithmetic  69.9 us
    ppermute x3, waiting for transfers between devices, sector_shape(): everything = lax.ppermute(everything, 'seq', ready)  58.7 us
    unnamed x143, local copies, waits for them, and re-layouts  44.5 us
    unnamed x1, blocking collectives  41.9 us
    dot_general x4, matrix products, transpose_dot(): lax.dot_general(left, right, (((0,), (0,)), ((), ())), preferred_element_...  34.4 us
  transfers between devices with their start and end apart: 9, of which 5 were waited for; matrix products, arithmetic and copies ran while one was open for 29% of the time, Pallas kernels for 0%

profile of v1, /device:TPU:0, one launch (start us, length us, event | category | flops | bytes accessed | tf_op | source)
XLA Modules:
  0.0 1462.6 jit_solution(15148836732180316506)
XLA Ops:
  15.8 9.0 reduce.48
  28.6 6.8 all-to-all-start.1
  36.8 8.3 convolution_add_fusion
  45.1 6.6 copy.101
  74.1 43.9 %collective-permute-done = bf16[1,512,768]{1,2,0:T(8,128)(2,1)} collective-permute-done((bf16[1,512,768]{1,2,0:T(8,128)(2,1)}, bf16[1,512,768]{1,2,0:T(8,128)(2,1)}, u32[]{:S(2)}, u32[]{:S(2)}) %collective-permute-start) | collective-permute-done | bytes 786464 | tf_op jit(solution)/shard_map/ppermute | solution.py:147
  120.1 14.8 %collective-permute-done.1 = bf16[1,512,768]{1,2,0:T(8,128)(2,1)} collective-permute-done((bf16[1,512,768]{1,2,0:T(8,128)(2,1)}, bf16[1,512,768]{1,2,0:T(8,128)(2,1)}, u32[]{:S(2)}, u32[]{:S(2)}) %collective-permute-start.1) | collective-permute-done | bytes 786464 | tf_op jit(solution)/shard_map/ppermute | solution.py:147
  167.8 10.6 fusion.177
  178.4 8.1 fusion
  186.5 8.0 fusion.130
  195.6 15.9 %fusion.181 = bf16[2048,1,256]{2,1,0:T(2,128)(2,1)} fusion(bf16[1,512,256]{2,0,1:T(2,128)(2,1)} %copy.109, bf16[1,512,256]{2,0,1:T(2,128)(2,1)} %copy.108, bf16[1,512,256]{2,0,1:T(2,128)(2,1)S(1)} %copy-done.22, bf16[1,512,256]{2,0,1:T(2,128)(2,1)S(1)} %copy-done.21), kind=kLoop, calls=%fused_computation.263 | loop fusion | flops 1572864 | bytes 2097152
  211.5 11.6 reduce.47
  275.7 7.1 multiply_convert_fusion.2
  292.2 9.2 multiply_reduce_fusion
  301.5 10.2 multiply_convert_fusion
  311.7 7.2 fusion.133
  349.7 8.4 fusion.71
  360.6 15.8 %copy.117 = bf16[1,2048,768]{2,0,1:T(2,128)(2,1)} copy(bf16[1,2048,768]{1,2,0:T(8,128)(2,1)} %bitcast.388) | data formatting | bytes 6291456 | tf_op jit(solution)/shard_map/convert_element_type | solution.py:263
  376.4 33.3 %reduce.49 = bf16[2048,768]{1,0:T(8,128)(2,1)} reduce(bf16[2048,1,768]{2,1,0:T(2,128)(2,1)} %bitcast.385, bf16[]{:T(256)} %broadcast.808), dimensions={1}, to_apply=%bitcast.310.reduce_sub_computation | reduce | bytes 6291458
  414.3 118.9 %all_to_all.39 = bf16[4,2,196608]{2,1,0:T(2,128)(2,1)} all-to-all(bf16[4,2,196608]{2,1,0:T(2,128)(2,1)} %reshape.1431), channel_id=1, replica_groups=mesh['dp'=8,'seq'=4] {'seq'}, dimensions={0} | all-to-all | bytes 6291456 | tf_op jit(solution)/shard_map/all_to_all | solution.py:266
  545.9 6.5 copy.119
  561.4 6.9 fusion.136
  569.0 28.1 %multiply_convert_fusion.3 = (bf16[512,4096]{1,0:T(8,128)(2,1)}, f32[512,4096]{1,0:T(8,128)}, f32[512,4096]{1,0:T(8,128)}) fusion(f32[4096]{0:T(1024)S(1)} %copy-done.40, bf16[1024,4096]{1,0:T(8,128)(2,1)} %param.45, bf16[1,512,1024]{2,1,0:T(8,128)(2,1)S(1)} %copy-done.12, f32[1024]{0:T(1024)S(1)} %copy-done.44, f32[1024]{0:T(1024)S(1)} %copy-done.36, ...), kind=kOutput, calls=%fused_computation.25 | convolution fusion | flops 4436525056 | bytes 30437376 | tf_op jit(solution)/shard_map/dot_general | solution.py:188
  597.1 14.5 convert_reduce_fusion
  613.6 8.7 fusion.171
  622.6 14.0 fusion.164
  636.6 10.7 fusion.183
  647.4 7.4 fusion.182
  657.2 9.3 fusion.87
  669.1 41.9 %all-reduce.13 = (f32[1024]{0:T(1024)S(1)}, f32[1024]{0:T(1024)S(1)}, f32[1024]{0:T(1024)S(1)}, f32[1024]{0:T(1024)S(1)}, f32[3072]{0:T(1024)S(1)}, /*index=5*/f32[1024]{0:T(1024)S(1)}, f32[4096]{0:T(1024)S(1)}) all-reduce(f32[1024]{0:T(1024)S(1)} %get-tuple-element.128, ...), channel_id=2, replica_groups=mesh['dp'=8,'seq'=4] {'dp','seq'}, use_global_device_ids=true, to_apply=%region_23.24.clone | all-reduce | flops 12288 | bytes 98304
  714.6 9.4 reduce-scatter.5.cloned.1.call-done
  724.0 366.3 %reduce-scatter.9.cloned.1.call-done = f32[32,4096]{1,0:T(8,128)} async-done(((f32[1024,4096]{1,0:T(8,128)}), f32[32,4096]{1,0:T(8,128)}) %reduce-scatter.9.cloned.1.call-update) | async-done | bytes 524304 | tf_op jit(solution)/shard_map/reduce_scatter | solution.py:304
  1090.3 365.0 %reduce-scatter.11.cloned.1.call-done = f32[128,1024]{1,0:T(8,128)} async-done(((f32[4096,1024]{1,0:T(8,128)}), f32[128,1024]{1,0:T(8,128)}) %reduce-scatter.11.cloned.1.call-update) | async-done | bytes 524304 | tf_op jit(solution)/shard_map/reduce_scatter | solution.py:306
  (253 shorter events, 204.9 us)
Async XLA Ops:
  15.3 20.1 %copy-start.47 = (s32[1,8]{1,0:T(1,128)S(1)}, s32[1,8]{1,0:T(1,128)}, u32[]{:S(2)}) copy-start(s32[1,8]{1,0:T(1,128)} %param.36) | copy-start | bytes 100
  15.3 20.2 %copy-start.11 = (bf16[1,512,1024]{2,1,0:T(8,128)(2,1)S(1)}, bf16[1,512,1024]{2,1,0:T(8,128)(2,1)}, u32[]{:S(2)}) copy-start(bf16[1,512,1024]{2,1,0:T(8,128)(2,1)} %param.35) | copy-start | bytes 3145732
  15.8 21.0 %copy-start.37 = (f32[1024]{0:T(1024)S(1)}, f32[1024]{0:T(1024)}, u32[]{:S(2)}) copy-start(f32[1024]{0:T(1024)} %param.37) | copy-start | bytes 12292
  15.8 21.0 %copy-start.41 = (f32[3072]{0:T(1024)S(1)}, f32[3072]{0:T(1024)}, u32[]{:S(2)}) copy-start(f32[3072]{0:T(1024)} %param.42) | copy-start | bytes 36868
  15.8 21.0 %copy-start.42 = (f32[1024]{0:T(1024)S(1)}, f32[1024]{0:T(1024)}, u32[]{:S(2)}) copy-start(f32[1024]{0:T(1024)} %param.38) | copy-start | bytes 12292
  28.6 196.3 %all-to-all-start.1 = ((bf16[4,2,65536]{2,1,0:T(2,128)(2,1)}), bf16[4,2,65536]{2,1,0:T(2,128)(2,1)}, u32[]{:S(2)}, u32[]{:S(2)}) async-start(bf16[4,2,65536]{2,1,0:T(2,128)(2,1)} %reshape.1429), calls=%async_computation.1 | async-start | bytes 2097152 | tf_op jit(solution)/shard_map/all_to_all | solution.py:204
  64.0 73.0 %collective-permute-start.2 = (bf16[1,512,768]{1,2,0:T(8,128)(2,1)S(1)}, bf16[1,512,768]{1,2,0:T(8,128)(2,1)}, u32[]{:S(2)}, u32[]{:S(2)}) collective-permute-start(bf16[1,512,768]{1,2,0:T(8,128)(2,1)S(1)} %get-tuple-element.156), channel_id=1, source_target_pairs={{0,3},{1,2},{2,1},{3,0},{4,7},{5,6},{6,5},{7,4},{8,11},{9,10},{10,... | collective-permute-start | bytes 2359304 | tf_op jit(solution)/shard_map/ppermute | solution.py:147
  67.9 67.0 %collective-permute-start.1 = (bf16[1,512,768]{1,2,0:T(8,128)(2,1)}, bf16[1,512,768]{1,2,0:T(8,128)(2,1)}, u32[]{:S(2)}, u32[]{:S(2)}) collective-permute-start(bf16[1,512,768]{1,2,0:T(8,128)(2,1)} %get-tuple-element.157), channel_id=1, source_target_pairs={{0,2},{1,3},{2,0},{3,1},{4,6},{5,7},{6,4},{7,5},{8,10},{9,11},{10,... | collective-permute-start | bytes 2359304 | tf_op jit(solution)/shard_map/ppermute | solution.py:147
  67.9 50.1 %collective-permute-start = (bf16[1,512,768]{1,2,0:T(8,128)(2,1)}, bf16[1,512,768]{1,2,0:T(8,128)(2,1)}, u32[]{:S(2)}, u32[]{:S(2)}) collective-permute-start(bf16[1,512,768]{1,2,0:T(8,128)(2,1)} %get-tuple-element.158), channel_id=1, source_target_pairs={{0,1},{1,0},{2,3},{3,2},{4,5},{5,4},{6,7},{7,6},{8,9},{9,8},{10,11... | collective-permute-start | bytes 2359304 | tf_op jit(solution)/shard_map/ppermute | solution.py:147
  141.3 19.5 %copy-start.13 = (bf16[1,2048,4,64]{1,3,2,0:T(8,128)(2,1)}, bf16[1,2048,4,64]{1,3,2,0:T(8,128)(2,1)S(1)}, u32[]{:S(2)}) copy-start(bf16[1,2048,4,64]{1,3,2,0:T(8,128)(2,1)S(1)} %get-tuple-element.153) | copy-start | bytes 3145732
  186.5 9.1 copy-start.21
  186.5 9.1 copy-start.22
  224.9 109.7 %all-to-all-start = ((bf16[4,2,65536]{2,1,0:T(2,128)(2,1)}), bf16[4,2,65536]{2,1,0:T(2,128)(2,1)}, u32[]{:S(2)}, u32[]{:S(2)}) async-start(bf16[4,2,65536]{2,1,0:T(2,128)(2,1)} %reshape.1427), calls=%async_computation | async-start | bytes 2097152 | tf_op jit(solution)/shard_map/all_to_all | solution.py:182
  229.2 485.4 %reduce-scatter.7.cloned.1.call-start = ((), (), s32[]{:S(2)}) async-start(), calls=%async_computation.8 | async-start | bytes 4325376 | tf_op jit(solution)/shard_map/reduce_scatter | solution.py:302
  239.1 22.2 %copy-start.9 = (bf16[1,2048,4,64]{1,3,2,0:T(8,128)(2,1)}, bf16[1,2048,4,64]{1,3,2,0:T(8,128)(2,1)S(1)}, u32[]{:S(2)}) copy-start(bf16[1,2048,4,64]{1,3,2,0:T(8,128)(2,1)S(1)} %reshape.1415) | copy-start | bytes 3145732
  275.7 16.5 %slice-start = ((s8[16777216]{0:T(1024)(128)(4,1)}), s8[4194304]{0:T(1024)(128)(4,1)S(1)}, s32[]{:S(2)}) async-start(s8[16777216]{0:T(1024)(128)(4,1)} %bitcast.373), calls=%async_computation.11 | async-start | bytes 8388608
  275.7 16.5 %slice-start.1 = ((s8[16777216]{0:T(1024)(128)(4,1)}), s8[4194304]{0:T(1024)(128)(4,1)S(1)}, s32[]{:S(2)}) async-start(s8[16777216]{0:T(1024)(128)(4,1)} %bitcast.373), calls=%async_computation.12 | async-start | bytes 8388608
  275.7 16.5 %slice-start.2 = ((s8[16777216]{0:T(1024)(128)(4,1)}), s8[4194304]{0:T(1024)(128)(4,1)S(1)}, s32[]{:S(2)}) async-start(s8[16777216]{0:T(1024)(128)(4,1)} %bitcast.373), calls=%async_computation.13 | async-start | bytes 8388608
  282.8 9.4 slice-start.3
  311.7 14.7 %copy-start.3 = (bf16[4,512,2048]{2,1,0:T(8,128)(2,1)S(1)}, bf16[4,512,2048]{2,1,0:T(8,128)(2,1)}, u32[]{:S(2)}) copy-start(bf16[4,512,2048]{2,1,0:T(8,128)(2,1)} %multiply_convert_fusion) | copy-start | bytes 25165828
  311.7 14.7 %copy-start.7 = (f32[1,2048,4,64]{1,3,2,0:T(8,128)S(1)}, f32[1,2048,4,64]{1,3,2,0:T(8,128)}, u32[]{:S(2)}) copy-start(f32[1,2048,4,64]{1,3,2,0:T(8,128)} %fusion.36) | copy-start | bytes 6291460
  311.7 18.4 %slice-start.7 = ((s8[12582912]{0:T(1024)(128)(4,1)}), s8[4194304]{0:T(1024)(128)(4,1)S(1)}, s32[]{:S(2)}) async-start(s8[12582912]{0:T(1024)(128)(4,1)} %bitcast.377), calls=%async_computation.18 | async-start | bytes 8388608
  319.0 11.2 slice-start.8
  334.6 9.0 copy-start.33
  348.4 375.6 %reduce-scatter.5.cloned.1.call-start = ((), (), s32[]{:S(2)}) async-start(), calls=%async_computation.7 | async-start | bytes 12976128 | tf_op jit(solution)/shard_map/reduce_scatter | solution.py:300
  568.3 522.1 %reduce-scatter.9.cloned.1.call-start = ((), (), s32[]{:S(2)}) async-start(), calls=%async_computation.9 | async-start | bytes 17301504 | tf_op jit(solution)/shard_map/reduce_scatter | solution.py:304
  569.0 28.1 %copy-start.24 = (bf16[1,512,1024]{2,1,0:T(8,128)(2,1)S(1)}, bf16[1,512,1024]{2,1,0:T(8,128)(2,1)}, u32[]{:S(2)}) copy-start(bf16[1,512,1024]{2,1,0:T(8,128)(2,1)} %param.49) | copy-start | bytes 3145732
  622.4 833.0 %reduce-scatter.11.cloned.1.call-start = ((), (), s32[]{:S(2)}) async-start(), calls=%async_computation.10 | async-start | bytes 17301504 | tf_op jit(solution)/shard_map/reduce_scatter | solution.py:306
  636.6 10.8 copy-start.49
  657.2 9.3 copy-start.20
  657.2 9.3 copy-start.25
  711.7 744.2 %copy-start.48 = (f32[32]{0:T(128)}, f32[32]{0:T(128)S(1)}, u32[]{:S(2)}) copy-start(f32[32]{0:T(128)S(1)} %dynamic-slice.67) | copy-start | bytes 388
  (40 other events, 142.5 us)
Sparse Core Ops, SparseCore 0:
  348.5 176.7 reduce-scatter.6
  568.4 155.5 reduce-scatter.4
  727.0 363.3 reduce-scatter.8
  1093.2 362.1 reduce-scatter.10
